TPU v7x, 128 devices: a whole 4x4x4 slice. The times are simulated.
128 devices in a mesh: ctx: 16 (over y, x), tp: 8 (over z, core).
Axes of the slice: x: 4, y: 4, z: 4, core: 2. Of those that a mesh axis runs over, the one named last changes fastest.
Arguments:
- ssm_input: bfloat16 [4096, 8192], P('ctx', 'tp'), may hold values from -6 to 6
- dt_raw: float32 [4096, 128], P('ctx', 'tp'), may hold values from -5 to 5
- b_proj: bfloat16 [4096, 8, 256], P('ctx', 'tp'), may hold values from -0.59765625 to 0.59765625
- c_proj: bfloat16 [4096, 8, 256], P('ctx', 'tp'), may hold values from -0.59765625 to 0.59765625
- dt_bias: float32 [128], P('tp'), may hold values from -1.5 to 0.5
- decay_rate: float32 [128], P('tp'), may hold values from 0.0002 to 0.05
- skip_gain: float32 [128], P('tp'), may hold values from 0.5 to 1.5
- doc_start: int32 [4096], P('ctx'), may hold values 0 or 1
- out_weight: bfloat16 [8192, 8192], P('tp'), may hold values from -0.0625 to 0.0625
- grad_out: bfloat16 [4096, 8192], P(('ctx', 'tp')), may hold values from -6 to 6
Outputs:
- layer_out: bfloat16 [4096, 8192], P(('ctx', 'tp'))
- grad_input: bfloat16 [4096, 8192], P('ctx', 'tp')
- grad_dt: float32 [4096, 128], P('ctx', 'tp')
- grad_b: bfloat16 [4096, 8, 256], P('ctx', 'tp')
- grad_c: bfloat16 [4096, 8, 256], P('ctx', 'tp')
- weight_grad: bfloat16 [8192, 8192], P('ctx', 'tp')
Inputs may be any that keep to these rules, and one draw needn't show every extreme that they name: `doc_start`: 1 marks the first token of a document; a document runs on until the next 1, across slabs.
All inputs are finite; a program needn't handle non-finite values. No bound on the sum of `doc_start` on one device may be relied on, other than what follows from the above.
Results may differ from a plain program's by a relative error of at most 0.022.
Values may be sent and summed in bfloat16 or wider, within the bound.
No kernel may reach another device: no remote copies, remote signals or barrier semaphores. Data moves between devices by JAX's collectives and lax.ppermute only.
A program may use at most 256 MiB of HBM per device.

v0:
```python
import jax
import jax.numpy as jnp
from jax import lax
from jax.sharding import PartitionSpec as P

HIGHEST = lax.Precision.HIGHEST


def prefix(value, axis, combine, identity, reverse):
    devices, mine = (lax.axis_size(axis), lax.axis_index(axis))
    everything = jax.tree.map(
        lambda part, kind: lax.all_gather(part.astype(kind), axis),
        value,
        (jnp.bfloat16, jnp.bfloat16),
    )
    start = jax.tree.map(
        lambda part, zero: jnp.broadcast_to(jnp.asarray(zero, part.dtype), part.shape),
        value,
        identity,
    )

    def step(k, before):
        at = devices - 1 - k if reverse else k
        reached = at > mine if reverse else at < mine
        new = combine(
            before, jax.tree.map(lambda part, own: part[at].astype(own.dtype), everything, value)
        )
        return jax.tree.map(lambda a, b: jnp.where(reached, a, b), new, before)

    return lax.fori_loop(0, devices, step, start)


def block_ssd(
    seq_in, step_raw, b_rows, c_rows, scores, carried, doc_start, bias_heads, rate_heads, skip_heads
):
    length = seq_in.shape[0]
    step_size = jax.nn.softplus(step_raw + bias_heads)
    cumul = jnp.cumsum(-step_size * rate_heads, axis=0)
    segment = jnp.cumsum(doc_start)
    reach = (segment == 0).astype(jnp.float32)
    order = jnp.arange(length)
    causal = (segment[:, None] == segment[None, :]) & (order[:, None] >= order[None, :])
    cum_heads = jnp.transpose(cumul, (1, 2, 0))
    differ = cum_heads[:, :, :, None] - cum_heads[:, :, None, :]
    decays = jnp.exp(jnp.where(causal, differ, -jnp.inf))
    mixing = decays * scores[:, None] * jnp.transpose(step_size, (1, 2, 0))[:, :, None, :]
    inside = jnp.einsum("gkts,sgkp->tgkp", mixing, seq_in, precision=HIGHEST)
    entry = jnp.exp(cumul) * reach[:, None, None]
    from_carry = entry[..., None] * jnp.einsum("tgn,gkpn->tgkp", c_rows, carried, precision=HIGHEST)
    mixer = inside + from_carry + skip_heads[..., None] * seq_in
    same_last = (segment == segment[-1]).astype(jnp.float32)
    tail = jnp.exp(cumul[-1] - cumul) * same_last[:, None, None] * step_size
    local_state = jnp.einsum("sgk,sgkp,sgn->gkpn", tail, seq_in, b_rows, precision=HIGHEST)
    through = reach[-1] * jnp.exp(cumul[-1])
    return (mixer, local_state, through)


def chain_combine(earlier, later):
    return (earlier[0] * later[0], later[0][..., None, None] * earlier[1] + later[1])


def shards(
    ssm_input,
    dt_raw,
    b_proj,
    c_proj,
    dt_bias,
    decay_rate,
    skip_gain,
    doc_start,
    out_weight,
    grad_out,
):
    rows = ssm_input.shape[0]
    heads = dt_raw.shape[1]
    head_dim = ssm_input.shape[1] // heads
    seq_f32 = ssm_input.astype(jnp.float32).reshape(rows, 1, heads, head_dim)
    step_raw = dt_raw.reshape(rows, 1, heads)
    b_rows = b_proj.astype(jnp.float32)
    c_rows = c_proj.astype(jnp.float32)
    bias_heads = dt_bias.reshape(1, heads)
    rate_heads = decay_rate.reshape(1, heads)
    skip_heads = skip_gain.reshape(1, heads)
    scores = jnp.einsum("tgn,sgn->gts", c_proj, b_proj, preferred_element_type=jnp.float32)
    step_size = jax.nn.softplus(step_raw + bias_heads)
    cumul = jnp.cumsum(-step_size * rate_heads, axis=0)
    segment = jnp.cumsum(doc_start)
    reach = (segment == 0).astype(jnp.float32)
    same_last = (segment == segment[-1]).astype(jnp.float32)
    tail = jnp.exp(cumul[-1] - cumul) * same_last[:, None, None] * step_size
    local_state = jnp.einsum("sgk,sgkp,sgn->gkpn", tail, seq_f32, b_rows, precision=HIGHEST)
    through = reach[-1] * jnp.exp(cumul[-1])
    identity_pair = (jnp.ones_like(through), jnp.zeros_like(local_state))
    carried = prefix((through, local_state), "ctx", chain_combine, identity_pair, False)[1]

    def local_fn(seq_arg, step_arg, b_arg, c_arg, score_arg):
        return block_ssd(
            seq_arg,
            step_arg,
            b_arg,
            c_arg,
            score_arg,
            carried,
            doc_start,
            bias_heads,
            rate_heads,
            skip_heads,
        )

    (mixer, _, _), pullback = jax.vjp(local_fn, seq_f32, step_raw, b_rows, c_rows, scores)
    mixer_bf = mixer.reshape(rows, heads * head_dim).astype(jnp.bfloat16)
    layer_out = lax.psum_scatter(
        jnp.dot(mixer_bf, out_weight, preferred_element_type=jnp.float32).astype(jnp.bfloat16),
        "tp",
        scatter_dimension=0,
        tiled=True,
    )
    grad_full = lax.all_gather(grad_out, "tp", axis=0, tiled=True)
    grad_mix = lax.dot_general(
        grad_full, out_weight, (((1,), (1,)), ((), ())), preferred_element_type=jnp.float32
    ).astype(jnp.bfloat16)
    grad_heads = grad_mix.astype(jnp.float32).reshape(rows, 1, heads, head_dim)
    entry = jnp.exp(cumul) * reach[:, None, None]
    local_grad = jnp.einsum("tgk,tgkp,tgn->gkpn", entry, grad_heads, c_rows, precision=HIGHEST)
    grad_next = prefix((through, local_grad), "ctx", chain_combine, identity_pair, True)[1]
    through_grad = jnp.sum(grad_next * carried, axis=(2, 3))
    grad_seq, grad_step, grad_brows, grad_crows, grad_scores = pullback(
        (grad_heads, grad_next, through_grad)
    )
    grad_brows = grad_brows + jnp.einsum("gts,tgn->sgn", grad_scores, c_rows, precision=HIGHEST)
    grad_crows = grad_crows + jnp.einsum("gts,sgn->tgn", grad_scores, b_rows, precision=HIGHEST)
    weight_sum = lax.psum_scatter(
        lax.dot_general(
            grad_full, mixer_bf, (((0,), (0,)), ((), ())), preferred_element_type=jnp.float32
        ).astype(jnp.bfloat16),
        "ctx",
        scatter_dimension=0,
        tiled=True,
    )
    return (
        layer_out,
        grad_seq.reshape(rows, heads * head_dim).astype(jnp.bfloat16),
        grad_step.reshape(rows, heads),
        grad_brows.astype(jnp.bfloat16),
        grad_crows.astype(jnp.bfloat16),
        weight_sum,
    )


def solution(mesh):
    in_specs = (
        P("ctx", "tp"),
        P("ctx", "tp"),
        P("ctx", "tp", None),
        P("ctx", "tp", None),
        P("tp"),
        P("tp"),
        P("tp"),
        P("ctx"),
        P("tp", None),
        P(("ctx", "tp"), None),
    )
    out_specs = (
        P(("ctx", "tp"), None),
        P("ctx", "tp"),
        P("ctx", "tp"),
        P("ctx", "tp", None),
        P("ctx", "tp", None),
        P("ctx", "tp"),
    )
    return jax.shard_map(shards, mesh=mesh, in_specs=in_specs, out_specs=out_specs, check_vma=False)
```

profile of v0, /device:TPU:0, one launch (start us, length us, event | category | flops | bytes accessed | tf_op | source)
XLA Modules:
  0.0 452.5 jit_solution(1089252134521595264)
XLA Ops:
  12.2 32.3 %all-gather.6.cloned.1.call-done = bf16[256,8192]{1,0:T(8,128)(2,1)} async-done(((bf16[32,8192]{1,0:T(8,128)(2,1)}), bf16[256,8192]{1,0:T(8,128)(2,1)}) %all-gather.6.cloned.1.call-update) | async-done | bytes 4194320 | tf_op jit(solution)/shard_map/all_gather | solution.py:118
  44.6 11.6 %convolution_convert_fusion.3 = bf16[256,1024]{1,0:T(8,128)(2,1)S(1)} fusion(bf16[256,8192]{1,0:T(8,128)(2,1)} %all-gather.6.cloned.1.call-done, bf16[1024,8192]{1,0:T(8,128)(2,1)} %param.22), kind=kOutput, calls=%fused_computation.43 | convolution fusion | flops 4295229440 | bytes 21495808 | tf_op jit(solution)/shard_map/dot_general | solution.py:119
  56.4 1.4 convolution_convert_fusion.1
  60.6 22.2 %all_gather.21 = bf16[16,1,16]{2,1,0:T(2,128)(2,1)} all-gather(bf16[1,1,16]{2,1,0:T(2,128)(2,1)S(1)} %get-tuple-element.399), channel_id=1, replica_groups=mesh['ctx'=16,'tp'=8] {'ctx'}, dimensions={0}, use_global_device_ids=true | all-gather | bytes 544 | tf_op jit(solution)/shard_map/all_gather | solution.py:12
  82.8 1.9 compare_convert_fusion
  84.7 43.8 %all-gather.10.cloned.1.call-done = bf16[256,64,256]{2,1,0:T(8,128)(2,1)} async-done(((bf16[16,64,256]{2,1,0:T(8,128)(2,1)}), bf16[256,64,256]{2,1,0:T(8,128)(2,1)}) %all-gather.10.cloned.1.call-update) | async-done | bytes 8388624 | tf_op jit(solution)/shard_map/all_gather | solution.py:12
  128.5 31.4 %while.31 = (s32[]{:T(128)}, f32[1,16,64,256]{3,2,1,0:T(8,128)S(1)}, s32[]{:T(128)}, bf16[16,1,16]{2,1,0:T(2,128)(2,1)}, bf16[16,1,16,64,256]{4,3,2,1,0:T(8,128)...) while((s32[]{:T(128)}, f32[1,16,64,256]{3,2,1,0:T(8,128)S(1)}, s32[]{:T(128)}, ...), condition=%wide.region_8.9_spmd.clone, body=%wide.region_7.8_spmd.clone.sunk | while | flops 1310744 | bytes 2621775 | solution.py:30
  129.2 1.3 fusion.99
  148.7 1.3 fusion.99
  150.6 1.3 fusion.99
  154.6 1.3 fusion.99
  159.9 2.2 fusion.50
  162.1 1.5 copy.170
  163.5 1.6 multiply_multiply_fusion
  165.8 1.7 multiply_reduce_fusion.4
  168.2 1.4 fusion.75
  169.7 1.6 copy.146
  171.2 2.2 convolution_convert_fusion.2
  176.5 1.3 bitcast_add_fusion.2
  177.8 1.5 fusion.62
  180.2 1.6 copy.140
  181.8 62.1 %all-gather.8.cloned.1.call-done = bf16[256,64,256]{2,1,0:T(8,128)(2,1)} async-done(((bf16[16,64,256]{2,1,0:T(8,128)(2,1)}), bf16[256,64,256]{2,1,0:T(8,128)(2,1)}) %all-gather.8.cloned.1.call-update) | async-done | bytes 8388624 | tf_op jit(solution)/shard_map/all_gather | solution.py:12
  243.9 31.2 %while.30 = (s32[]{:T(128)}, f32[1,16,64,256]{3,2,1,0:T(8,128)S(1)}, s32[]{:T(128)}, bf16[16,1,16]{2,1,0:T(2,128)(2,1)}, bf16[16,1,16,64,256]{4,3,2,1,0:T(8,128)(2,1)}, /*index=5*/s32[]{:T(128)}, s32[]{:T(128)}) while((s32[]{:T(128)}, f32[1,16,64,256]{3,2,1,0:T(8,128)S(1)}, s32[]{:T(128)}, bf16[16,1,16]{2,1,0:T(2,128)(2,1)}, ...), condition=%wide.region_5.6_spmd.clone, body=%wide.region_4.5_spmd.clone.sunk | while | flops 1310740 | bytes 2621713 | solution.py:30
  244.6 1.3 fusion.98
  260.2 1.3 fusion.98
  264.1 1.3 fusion.98
  276.4 5.8 %fusion.40 = bf16[256,1,16,64]{0,3,2,1:T(8,128)(2,1)} fusion(bf16[256,16,64]{0,2,1:T(8,128)(2,1)} %bitcast.245, f32[16,256]{1,0:T(8,128)} %copy.140, f32[256,256]{1,0:T(8,128)} %fusion.77, f32[16,256]{1,0:T(8,128)} %bitcast_add_fusion.2, pred[256,256]{1,0:T(8,128)(4,1)} %fusion.62, f32[256,1,16,64]{0,3,2,1:T(8,128)} %bitcast.256, ...), kind=kOutput, calls=%fused_computation.42 | convolution fusion | flops 810811392 | bytes 3522624 | tf_op jit(solution)/shard_map/jvp(gkts,sgkp->tgkp)/dot_general | solution.py:47
  282.2 12.6 %convert_bitcast_fusion = bf16[8192,1024]{0,1:T(8,128)(2,1)} fusion(bf16[256,1024]{0,1:T(8,128)(2,1)} %bitcast.248, bf16[256,8192]{1,0:T(8,128)(2,1)} %all-gather.6.cloned.1.call-done), kind=kOutput, calls=%fused_computation.6 | convolution fusion | flops 4303355904 | bytes 21495808 | tf_op jit(solution)/shard_map/dot_general | solution.py:133
  295.1 12.5 %convolution_convert_fusion = bf16[256,8192]{1,0:T(8,128)(2,1)} fusion(bf16[256,1024]{0,1:T(8,128)(2,1)} %bitcast.249, bf16[1024,8192]{1,0:T(8,128)(2,1)} %param.22), kind=kOutput, calls=%fused_computation.7 | convolution fusion | flops 4297064448 | bytes 21495808 | tf_op jit(solution)/shard_map/dot_general | solution.py:113
  307.6 2.1 copy.152
  309.7 5.2 %fusion.37 = bf16[256,1,16,64]{0,3,2,1:T(8,128)(2,1)} fusion(bf16[16,64,256]{2,1,0:T(8,128)(2,1)} %bitcast.260, f32[16,256]{1,0:T(8,128)} %copy.140, f32[256,256]{1,0:T(8,128)} %fusion.77, f32[16,256]{1,0:T(8,128)} %bitcast_add_fusion.2, pred[256,256]{1,0:T(8,128)(4,1)} %fusion.62, f32[256,16,64]{0,2,1:T(8,128)S(1)} %bitcast.242, ...), kind=kOutput, calls=%fused_computation.39 | convolution fusion | flops 810811392 | bytes 3522624 | tf_op jit(solution)/shard_map/transpose(jvp(gkts,sgkp->tgkp))/dot_general | solution.py:47
  314.8 2.0 copy.162
  316.9 5.2 %fusion.9 = (f32[16,256]{1,0:T(8,128)}, f32[16,256]{1,0:T(8,128)}, f32[16,256]{1,0:T(8,128)}, f32[256,256]{1,0:T(8,128)}) fusion(f32[16,256]{1,0:T(8,128)} %copy.140, f32[256,256]{1,0:T(8,128)} %fusion.77, f32[16,256]{1,0:T(8,128)} %bitcast_add_fusion.2, pred[256,256]{1,0:T(8,128)(4,1)} %fusion.62, bf16[16,64,256]{2,1,0:T(8,128)(2,1)} %bitcast.261, ...), kind=kOutput, calls=%fused_computation.17 | convolution fusion | flops 147771392 | bytes 1720320 | tf_op jit(solution)/shard_map/transpose(jvp(gkts,sgkp->tgkp))/dot_general | solution.py:47
  322.1 1.5 copy.156
  323.6 1.5 copy.157
  325.0 1.5 copy.153
  326.5 2.9 fusion.44
  329.4 1.9 fusion.49
  331.3 1.7 copy.164
  333.0 1.9 convolution_bitcast_fusion.2
  335.9 1.5 copy.155
  337.6 1.3 bitcast_multiply_fusion.2
  339.0 1.5 add_add_fusion
  340.5 2.5 reduce-window.29
  345.2 3.4 fusion.47
  348.6 56.6 %reduce-scatter.5.cloned.1.call-done = bf16[512,1024]{0,1:T(8,128)(2,1)} async-done(((bf16[8192,1024]{0,1:T(8,128)(2,1)}), bf16[512,1024]{0,1:T(8,128)(2,1)}) %reduce-scatter.5.cloned.1.call-update) | async-done | bytes 1048592 | tf_op jit(solution)/shard_map/reduce_scatter | solution.py:132
  405.2 2.3 copy.165
  407.4 38.5 %reduce-scatter.3.cloned.1.call-done = bf16[32,8192]{1,0:T(8,128)(2,1)} async-done(((bf16[256,8192]{1,0:T(8,128)(2,1)}), bf16[32,8192]{1,0:T(8,128)(2,1)}) %reduce-scatter.3.cloned.1.call-update) | async-done | bytes 524304 | tf_op jit(solution)/shard_map/reduce_scatter | solution.py:112
  (133 shorter events, 71.0 us)
Async XLA Ops:
  7.2 49.2 %copy-start = (bf16[256,1,256]{2,0,1:T(8,128)(2,1)S(1)}, bf16[256,1,256]{2,0,1:T(8,128)(2,1)}, u32[]{:S(2)}) copy-start(bf16[256,1,256]{2,0,1:T(8,128)(2,1)} %param.17) | copy-start | bytes 393220
  7.2 37.4 %all-gather.6.cloned.1.call-start = ((), (), s32[]{:S(2)}) async-start(), calls=%async_computation.3 | async-start | bytes 4718592 | tf_op jit(solution)/shard_map/all_gather | solution.py:118
  7.9 120.5 %all-gather.10.cloned.1.call-start = ((), (), s32[]{:S(2)}) async-start(), calls=%async_computation.6 | async-start | bytes 8912896 | tf_op jit(solution)/shard_map/all_gather | solution.py:12
  11.8 46.1 %copy-start.12 = (f32[256]{0:T(256)}, f32[256]{0:T(256)S(1)}, u32[]{:S(2)}) copy-start(f32[256]{0:T(256)S(1)} %get-tuple-element.392) | copy-start | bytes 3076
  11.8 46.8 %copy-start.11 = (s32[256]{0:T(256)}, s32[256]{0:T(256)S(1)}, u32[]{:S(2)}) copy-start(s32[256]{0:T(256)S(1)} %get-tuple-element.393) | copy-start | bytes 3076
  11.8 32.8 %copy-start.8 = (f32[16,2,128]{0,2,1:T(8,128)}, f32[16,2,128]{0,2,1:T(8,128)S(1)}, u32[]{:S(2)}) copy-start(f32[16,2,128]{0,2,1:T(8,128)S(1)} %broadcast.148) | copy-start | bytes 49156
  12.2 47.2 %copy-start.5 = (f32[256,1,16]{2,1,0:T(1,128)}, f32[256,1,16]{2,1,0:T(1,128)S(1)}, u32[]{:S(2)}) copy-start(f32[256,1,16]{2,1,0:T(1,128)S(1)} %get-tuple-element.391) | copy-start | bytes 49156
  12.2 44.1 %copy-start.9 = (f32[256,16]{0,1:T(8,128)}, f32[256,16]{0,1:T(8,128)S(1)}, u32[]{:S(2)}) copy-start(f32[256,16]{0,1:T(8,128)S(1)} %copy.144) | copy-start | bytes 49156
  56.1 1.8 copy-start.3
  56.1 3.0 copy-start.2
  57.8 186.1 %all-gather.8.cloned.1.call-start = ((), (), s32[]{:S(2)}) async-start(), calls=%async_computation.5 | async-start | bytes 8912896 | tf_op jit(solution)/shard_map/all_gather | solution.py:12
  59.4 111.9 %copy-start.1 = (bf16[256,1024]{0,1:T(8,128)(2,1)}, bf16[256,1024]{0,1:T(8,128)(2,1)S(1)}, u32[]{:S(2)}) copy-start(bf16[256,1024]{0,1:T(8,128)(2,1)S(1)} %copy.141) | copy-start | bytes 1572868
  128.5 31.4 %copy-start.4 = (bf16[256,1,256]{2,0,1:T(8,128)(2,1)S(1)}, bf16[256,1,256]{2,0,1:T(8,128)(2,1)}, u32[]{:S(2)}) copy-start(bf16[256,1,256]{2,0,1:T(8,128)(2,1)} %param.16) | copy-start | bytes 393220
  165.2 0.6 copy-start.7
  167.6 0.6 copy-start.6
  173.4 231.7 %reduce-scatter.5.cloned.1.call-start = ((), (), s32[]{:S(2)}) async-start(), calls=%async_computation.4 | async-start | bytes 17825792 | tf_op jit(solution)/shard_map/reduce_scatter | solution.py:132
  243.9 32.5 %copy-start.10 = (f32[256,16]{0,1:T(8,128)S(1)}, f32[256,16]{0,1:T(8,128)}, u32[]{:S(2)}) copy-start(f32[256,16]{0,1:T(8,128)} %copy-done.9) | copy-start | bytes 49156
  294.8 151.1 %reduce-scatter.3.cloned.1.call-start = ((), (), s32[]{:S(2)}) async-start(), calls=%async_computation.2 | async-start | bytes 4718592 | tf_op jit(solution)/shard_map/reduce_scatter | solution.py:112
Sparse Core Ops, SparseCore 0:
  9.7 34.7 all-gather.5
  58.0 70.4 all-gather.9
  173.6 70.3 all-gather.7
  295.0 110.1 reduce-scatter.4
  408.0 37.8 reduce-scatter.2
where the time goes:
time: 455 us; the launch traced here: 452 us
  waiting for transfers between devices  234 us (51%)
  other arithmetic  83.1 us (18%)
  matrix products  71 us (16%)
  local copies, waits for them, and re-layouts  26.8 us (6%)
  blocking collectives  22.2 us (5%)
  between operations  14 us (3%)
    all_gather x2, waiting for transfers between devices, prefix(): lax.all_gather(part.astype(kind), axis)  106 us
    reduce_scatter x1, waiting for transfers between devices, shards(): lax.psum_scatter(lax.dot_general(grad_full, mixer_bf, (((0,), (0,)), ((),...  56.6 us
    select_n x32, other arithmetic, step(): return jax.tree.map(lambda a, b: jnp.where(reached, a, b), new, before)  41.2 us
    reduce_scatter x1, waiting for transfers between devices, shards(): lax.psum_scatter(jnp.dot(mixer_bf, out_weight, preferred_element_type=jnp...  38.5 us
    all_gather x1, waiting for transfers between devices, shards(): grad_full = lax.all_gather(grad_out, 'tp', axis=0, tiled=True)  32.3 us
    all_gather x1, blocking collectives, prefix(): lax.all_gather(part.astype(kind), axis)  22.2 us
    convert_element_type x32, other arithmetic, step(): part[at].astype(own.dtype)  20.5 us
    dot_general x3, matrix products, block_ssd(): inside = jnp.einsum('gkts,sgkp->tgkp', mixing, seq_in, precision=HIGHEST)  16.2 us
  transfers between devices with their start and end apart: 5, of which 5 were waited for; matrix products, arithmetic and copies ran while one was open for 16% of the time, Pallas kernels for 0%

commit v1 on v0

--- a/solution.py
+++ b/solution.py
@@ -115,7 +115,9 @@
         scatter_dimension=0,
         tiled=True,
     )
-    grad_full = lax.all_gather(grad_out, "tp", axis=0, tiled=True)
+    grad_full = jnp.concatenate(
+        lax.all_to_all(jnp.stack([grad_out] * lax.axis_size("tp")), "tp", 0, 0), axis=0
+    )
     grad_mix = lax.dot_general(
         grad_full, out_weight, (((1,), (1,)), ((), ())), preferred_element_type=jnp.float32
     ).astype(jnp.bfloat16)

time: 455 us -> 477 us (1.048)
  waiting for transfers between devices: 234 us -> 247 us
  starting transfers between devices: 0.6 us -> 6.1 us
    all_to_all x0 -> x1, waiting for transfers between devices: none -> 46.9 us  [shards(): lax.all_to_all(jnp.stack([grad_out] * lax.axis_size('tp')), 'tp', 0, 0)]
    all_gather x1 -> x0, waiting for transfers between devices: 32.3 us -> none  [shards(): grad_full = lax.all_gather(grad_out, 'tp', axis=0, tiled=True)]
    all_to_all x0 -> x1, starting transfers between devices: none -> 5.54 us  [shards(): lax.all_to_all(jnp.stack([grad_out] * lax.axis_size('tp')), 'tp', 0, 0)]
  transfers between devices with their start and end apart: 5 -> 5, of which waited for: 5 -> 5; matrix products, arithmetic and copies ran while one was open for 16% -> 15% of each run, Pallas kernels for 0% -> 0%
where the time goes in v1:
time: 477 us; the launch traced here: 474 us
  waiting for transfers between devices  247 us (52%)
  other arithmetic  82.3 us (17%)
  matrix products  71 us (15%)
  local copies, waits for them, and re-layouts  30.2 us (6%)
  blocking collectives  22.5 us (5%)
  between operations  14 us (3%)
  starting transfers between devices  6.1 us (1%)
    all_gather x2, waiting for transfers between devices, prefix(): lax.all_gather(part.astype(kind), axis)  105 us
    reduce_scatter x1, waiting for transfers between devices, shards(): lax.psum_scatter(lax.dot_general(grad_full, mixer_bf, (((0,), (0,)), ((),...  56.6 us
    all_to_all x1, waiting for transfers between devices, shards(): lax.all_to_all(jnp.stack([grad_out] * lax.axis_size('tp')), 'tp', 0, 0)  46.9 us
    select_n x32, other arithmetic, step(): return jax.tree.map(lambda a, b: jnp.where(reached, a, b), new, before)  41.2 us
    reduce_scatter x1, waiting for transfers between devices, shards(): lax.psum_scatter(jnp.dot(mixer_bf, out_weight, preferred_element_type=jnp...  38.5 us
    all_gather x1, blocking collectives, prefix(): lax.all_gather(part.astype(kind), axis)  22.5 us
    convert_element_type x32, other arithmetic, step(): part[at].astype(own.dtype)  20.5 us
    dot_general x3, matrix products, block_ssd(): inside = jnp.einsum('gkts,sgkp->tgkp', mixing, seq_in, precision=HIGHEST)  16.2 us
  transfers between devices with their start and end apart: 5, of which 5 were waited for; matrix products, arithmetic and copies ran while one was open for 15% of the time, Pallas kernels for 0%

profile of v1, /device:TPU:0, one launch (start us, length us, event | category | flops | bytes accessed | tf_op | source)
XLA Modules:
  0.0 473.7 jit_solution(8474673955386111068)
XLA Ops:
  7.2 3.5 stack.2
  10.7 5.5 %all-to-all-start = ((bf16[8,32,8192]{2,1,0:T(8,128)(2,1)}), bf16[8,32,8192]{2,1,0:T(8,128)(2,1)}, u32[]{:S(2)}, u32[]{:S(2)}) async-start(bf16[8,32,8192]{2,1,0:T(8,128)(2,1)} %stack.2), calls=%async_computation.1 | async-start | bytes 8388608 | tf_op jit(solution)/shard_map/all_to_all | solution.py:119
  19.1 46.9 %all-to-all-done = bf16[8,32,8192]{2,1,0:T(8,128)(2,1)} async-done(((bf16[8,32,8192]{2,1,0:T(8,128)(2,1)}), bf16[8,32,8192]{2,1,0:T(8,128)(2,1)}, u32[]{:S(2)}, u32[]{:S(2)}) %all-to-all-start) | async-done | bytes 4194336 | tf_op jit(solution)/shard_map/all_to_all | solution.py:119
  66.0 11.6 %convolution_convert_fusion.3 = bf16[256,1024]{1,0:T(8,128)(2,1)S(1)} fusion(bf16[256,8192]{1,0:T(8,128)(2,1)} %bitcast.34, bf16[1024,8192]{1,0:T(8,128)(2,1)} %param.22), kind=kOutput, calls=%fused_computation.43 | convolution fusion | flops 4295229440 | bytes 21495808 | tf_op jit(solution)/shard_map/dot_general | solution.py:121
  77.8 1.4 convolution_convert_fusion.1
  82.7 22.5 %all_gather.18 = bf16[16,1,16]{2,1,0:T(2,128)(2,1)} all-gather(bf16[1,1,16]{2,1,0:T(2,128)(2,1)S(1)} %get-tuple-element.399), channel_id=1, replica_groups=mesh['ctx'=16,'tp'=8] {'ctx'}, dimensions={0}, use_global_device_ids=true | all-gather | bytes 544 | tf_op jit(solution)/shard_map/all_gather | solution.py:12
  105.2 1.9 compare_convert_fusion
  107.1 42.5 %all-gather.7.cloned.1.call-done = bf16[256,64,256]{2,1,0:T(8,128)(2,1)} async-done(((bf16[16,64,256]{2,1,0:T(8,128)(2,1)}), bf16[256,64,256]{2,1,0:T(8,128)(2,1)}) %all-gather.7.cloned.1.call-update) | async-done | bytes 8388624 | tf_op jit(solution)/shard_map/all_gather | solution.py:12
  149.7 31.4 %while.31 = (s32[]{:T(128)}, f32[1,16,64,256]{3,2,1,0:T(8,128)S(1)}, s32[]{:T(128)}, bf16[16,1,16]{2,1,0:T(2,128)(2,1)}, bf16[16,1,16,64,256]{4,3,2,1,0:T(8,128)...) while((s32[]{:T(128)}, f32[1,16,64,256]{3,2,1,0:T(8,128)S(1)}, s32[]{:T(128)}, ...), condition=%wide.region_8.9_spmd.clone, body=%wide.region_7.8_spmd.clone.sunk | while | flops 1310744 | bytes 2621775 | solution.py:30
  158.2 1.3 fusion.99
  169.9 1.3 fusion.99
  181.1 2.2 fusion.50
  183.3 1.5 copy.170
  184.7 1.6 multiply_multiply_fusion
  187.0 1.7 multiply_reduce_fusion.4
  189.4 1.4 fusion.75
  190.9 1.6 copy.146
  192.4 2.2 convolution_convert_fusion.2
  197.7 1.3 bitcast_add_fusion.2
  199.0 1.5 fusion.62
  201.4 1.6 copy.140
  203.0 62.1 %all-gather.5.cloned.1.call-done = bf16[256,64,256]{2,1,0:T(8,128)(2,1)} async-done(((bf16[16,64,256]{2,1,0:T(8,128)(2,1)}), bf16[256,64,256]{2,1,0:T(8,128)(2,1)}) %all-gather.5.cloned.1.call-update) | async-done | bytes 8388624 | tf_op jit(solution)/shard_map/all_gather | solution.py:12
  265.1 31.2 %while.30 = (s32[]{:T(128)}, f32[1,16,64,256]{3,2,1,0:T(8,128)S(1)}, s32[]{:T(128)}, bf16[16,1,16]{2,1,0:T(2,128)(2,1)}, bf16[16,1,16,64,256]{4,3,2,1,0:T(8,128)(2,1)}, /*index=5*/s32[]{:T(128)}, s32[]{:T(128)}) while((s32[]{:T(128)}, f32[1,16,64,256]{3,2,1,0:T(8,128)S(1)}, s32[]{:T(128)}, bf16[16,1,16]{2,1,0:T(2,128)(2,1)}, ...), condition=%wide.region_5.6_spmd.clone, body=%wide.region_4.5_spmd.clone.sunk | while | flops 1310740 | bytes 2621713 | solution.py:30
  269.7 1.3 fusion.98
  271.7 1.3 fusion.98
  273.6 1.3 fusion.98
  297.6 5.8 %fusion.40 = bf16[256,1,16,64]{0,3,2,1:T(8,128)(2,1)} fusion(bf16[256,16,64]{0,2,1:T(8,128)(2,1)} %bitcast.246, f32[16,256]{1,0:T(8,128)} %copy.140, f32[256,256]{1,0:T(8,128)} %fusion.77, f32[16,256]{1,0:T(8,128)} %bitcast_add_fusion.2, pred[256,256]{1,0:T(8,128)(4,1)} %fusion.62, f32[256,1,16,64]{0,3,2,1:T(8,128)} %bitcast.257, ...), kind=kOutput, calls=%fused_computation.42 | convolution fusion | flops 810811392 | bytes 3522624 | tf_op jit(solution)/shard_map/jvp(gkts,sgkp->tgkp)/dot_general | solution.py:47
  303.4 12.6 %convert_bitcast_fusion = bf16[8192,1024]{0,1:T(8,128)(2,1)} fusion(bf16[256,1024]{0,1:T(8,128)(2,1)} %bitcast.249, bf16[256,8192]{1,0:T(8,128)(2,1)} %bitcast.34), kind=kOutput, calls=%fused_computation.6 | convolution fusion | flops 4303355904 | bytes 21495808 | tf_op jit(solution)/shard_map/dot_general | solution.py:135
  316.3 12.5 %convolution_convert_fusion = bf16[256,8192]{1,0:T(8,128)(2,1)} fusion(bf16[256,1024]{0,1:T(8,128)(2,1)} %bitcast.250, bf16[1024,8192]{1,0:T(8,128)(2,1)} %param.22), kind=kOutput, calls=%fused_computation.7 | convolution fusion | flops 4297064448 | bytes 21495808 | tf_op jit(solution)/shard_map/dot_general | solution.py:113
  328.8 2.1 copy.152
  330.9 5.2 %fusion.37 = bf16[256,1,16,64]{0,3,2,1:T(8,128)(2,1)} fusion(bf16[16,64,256]{2,1,0:T(8,128)(2,1)} %bitcast.261, f32[16,256]{1,0:T(8,128)} %copy.140, f32[256,256]{1,0:T(8,128)} %fusion.77, f32[16,256]{1,0:T(8,128)} %bitcast_add_fusion.2, pred[256,256]{1,0:T(8,128)(4,1)} %fusion.62, f32[256,16,64]{0,2,1:T(8,128)S(1)} %bitcast.243, ...), kind=kOutput, calls=%fused_computation.39 | convolution fusion | flops 810811392 | bytes 3522624 | tf_op jit(solution)/shard_map/transpose(jvp(gkts,sgkp->tgkp))/dot_general | solution.py:47
  336.0 2.0 copy.162
  338.1 5.2 %fusion.9 = (f32[16,256]{1,0:T(8,128)}, f32[16,256]{1,0:T(8,128)}, f32[16,256]{1,0:T(8,128)}, f32[256,256]{1,0:T(8,128)}) fusion(f32[16,256]{1,0:T(8,128)} %copy.140, f32[256,256]{1,0:T(8,128)} %fusion.77, f32[16,256]{1,0:T(8,128)} %bitcast_add_fusion.2, pred[256,256]{1,0:T(8,128)(4,1)} %fusion.62, bf16[16,64,256]{2,1,0:T(8,128)(2,1)} %bitcast.262, ...), kind=kOutput, calls=%fused_computation.17 | convolution fusion | flops 147771392 | bytes 1720320 | tf_op jit(solution)/shard_map/transpose(jvp(gkts,sgkp->tgkp))/dot_general | solution.py:47
  343.3 1.5 copy.156
  344.8 1.5 copy.157
  346.2 1.5 copy.153
  347.7 2.9 fusion.44
  350.6 1.9 fusion.49
  352.5 1.7 copy.164
  354.2 1.9 convolution_bitcast_fusion.2
  357.1 1.5 copy.155
  358.8 1.4 bitcast_multiply_fusion.2
  360.1 1.5 add_add_fusion
  361.7 2.5 reduce-window.29
  366.3 3.5 fusion.47
  369.8 56.6 %reduce-scatter.5.cloned.1.call-done = bf16[512,1024]{0,1:T(8,128)(2,1)} async-done(((bf16[8192,1024]{0,1:T(8,128)(2,1)}), bf16[512,1024]{0,1:T(8,128)(2,1)}) %reduce-scatter.5.cloned.1.call-update) | async-done | bytes 1048592 | tf_op jit(solution)/shard_map/reduce_scatter | solution.py:134
  426.4 2.3 copy.165
  428.7 38.5 %reduce-scatter.3.cloned.1.call-done = bf16[32,8192]{1,0:T(8,128)(2,1)} async-done(((bf16[256,8192]{1,0:T(8,128)(2,1)}), bf16[32,8192]{1,0:T(8,128)(2,1)}) %reduce-scatter.3.cloned.1.call-update) | async-done | bytes 524304 | tf_op jit(solution)/shard_map/reduce_scatter | solution.py:112
  (139 shorter events, 72.0 us)
Async XLA Ops:
  7.2 70.7 %copy-start = (bf16[256,1,256]{2,0,1:T(8,128)(2,1)S(1)}, bf16[256,1,256]{2,0,1:T(8,128)(2,1)}, u32[]{:S(2)}) copy-start(bf16[256,1,256]{2,0,1:T(8,128)(2,1)} %param.17) | copy-start | bytes 393220
  10.7 5.6 %copy-start.15 = (s32[256]{0:T(256)S(1)}, s32[256]{0:T(256)}, u32[]{:S(2)}) copy-start(s32[256]{0:T(256)} %param.21) | copy-start | bytes 3076
  10.7 6.0 %copy-start.11 = (f32[256,16]{0,1:T(8,128)S(1)}, f32[256,16]{0,1:T(8,128)}, u32[]{:S(2)}) copy-start(f32[256,16]{0,1:T(8,128)} %param.15) | copy-start | bytes 49156
  10.7 6.1 %copy-start.13 = (f32[16]{0:T(128)S(1)}, f32[16]{0:T(128)}, u32[]{:S(2)}) copy-start(f32[16]{0:T(128)} %param.18) | copy-start | bytes 196
  10.7 6.1 %copy-start.14 = (f32[16]{0:T(128)S(1)}, f32[16]{0:T(128)}, u32[]{:S(2)}) copy-start(f32[16]{0:T(128)} %param.19) | copy-start | bytes 196
  10.7 55.3 %all-to-all-start = ((bf16[8,32,8192]{2,1,0:T(8,128)(2,1)}), bf16[8,32,8192]{2,1,0:T(8,128)(2,1)}, u32[]{:S(2)}, u32[]{:S(2)}) async-start(bf16[8,32,8192]{2,1,0:T(8,128)(2,1)} %stack.2), calls=%async_computation.1 | async-start | bytes 8388608 | tf_op jit(solution)/shard_map/all_to_all | solution.py:119
  16.2 133.4 %all-gather.7.cloned.1.call-start = ((), (), s32[]{:S(2)}) async-start(), calls=%async_computation.6 | async-start | bytes 8912896 | tf_op jit(solution)/shard_map/all_gather | solution.py:12
  18.7 60.7 %copy-start.12 = (f32[256]{0:T(256)}, f32[256]{0:T(256)S(1)}, u32[]{:S(2)}) copy-start(f32[256]{0:T(256)S(1)} %get-tuple-element.392) | copy-start | bytes 3076
  18.7 47.3 %copy-start.8 = (f32[16,2,128]{0,2,1:T(8,128)}, f32[16,2,128]{0,2,1:T(8,128)S(1)}, u32[]{:S(2)}) copy-start(f32[16,2,128]{0,2,1:T(8,128)S(1)} %broadcast.150) | copy-start | bytes 49156
  19.0 62.5 %copy-start.5 = (f32[256,1,16]{2,1,0:T(1,128)}, f32[256,1,16]{2,1,0:T(1,128)S(1)}, u32[]{:S(2)}) copy-start(f32[256,1,16]{2,1,0:T(1,128)S(1)} %get-tuple-element.391) | copy-start | bytes 49156
  19.1 58.7 %copy-start.9 = (f32[256,16]{0,1:T(8,128)}, f32[256,16]{0,1:T(8,128)S(1)}, u32[]{:S(2)}) copy-start(f32[256,16]{0,1:T(8,128)S(1)} %copy.144) | copy-start | bytes 49156
  77.6 2.4 copy-start.3
  77.6 3.7 copy-start.2
  79.3 185.8 %all-gather.5.cloned.1.call-start = ((), (), s32[]{:S(2)}) async-start(), calls=%async_computation.5 | async-start | bytes 8912896 | tf_op jit(solution)/shard_map/all_gather | solution.py:12
  81.5 111.0 %copy-start.1 = (bf16[256,1024]{0,1:T(8,128)(2,1)}, bf16[256,1024]{0,1:T(8,128)(2,1)S(1)}, u32[]{:S(2)}) copy-start(bf16[256,1024]{0,1:T(8,128)(2,1)S(1)} %copy.141) | copy-start | bytes 1572868
  149.7 31.4 %copy-start.4 = (bf16[256,1,256]{2,0,1:T(8,128)(2,1)S(1)}, bf16[256,1,256]{2,0,1:T(8,128)(2,1)}, u32[]{:S(2)}) copy-start(bf16[256,1,256]{2,0,1:T(8,128)(2,1)} %param.16) | copy-start | bytes 393220
  186.4 0.6 copy-start.7
  188.8 0.6 copy-start.6
  194.6 231.8 %reduce-scatter.5.cloned.1.call-start = ((), (), s32[]{:S(2)}) async-start(), calls=%async_computation.4 | async-start | bytes 17825792 | tf_op jit(solution)/shard_map/reduce_scatter | solution.py:134
  265.1 32.5 %copy-start.10 = (f32[256,16]{0,1:T(8,128)S(1)}, f32[256,16]{0,1:T(8,128)}, u32[]{:S(2)}) copy-start(f32[256,16]{0,1:T(8,128)} %copy-done.9) | copy-start | bytes 49156
  316.0 151.1 %reduce-scatter.3.cloned.1.call-start = ((), (), s32[]{:S(2)}) async-start(), calls=%async_computation.3 | async-start | bytes 4718592 | tf_op jit(solution)/shard_map/reduce_scatter | solution.py:112
Sparse Core Ops, SparseCore 0:
  79.4 70.2 all-gather.6
  194.8 70.3 all-gather.4
  316.2 110.1 reduce-scatter.4
  429.2 37.8 reduce-scatter.2
